TPU v7x, 512 devices: a whole 4x8x8 slice. The times are simulated.
512 devices in a mesh: dp: 32 (over x, y), segment: 2 (over core), mp: 8 (over z).
Axes of the slice: x: 4, y: 8, z: 8, core: 2. Of those that a mesh axis runs over, the one named last changes fastest.
Arguments:
- frames: bfloat16 [2, 8192, 1280], P(None, ('dp', 'mp')), may hold values from -8 to 8
- dec_states: bfloat16 [2, 2048, 1280], P(None, 'dp'), may hold values from -8 to 8
- out_grad: bfloat16 [2, 2048, 1280], P(None, 'dp'), may hold values from -3 to 3
- frame_lengths: int32 [2, 32, 4], P(None, 'dp'), may hold values from 1 to 128, 256 in all within a row
- token_lengths: int32 [2, 32, 4], P(None, 'dp'), may hold values from 1 to 32, 64 in all within a row
- weights: bfloat16 [2, 4, 1024, 1280], P('segment', None, 'mp'), may hold values from -1 to 1
- norm_gains: float32 [3, 1280], replicated, may hold values from 0.25 to 1.75
- norm_biases: float32 [3, 1280], replicated, may hold values from -2 to 2
Outputs:
- gradient: float32 [2, 3, 1024, 1280], P('segment', None, 'mp')
Inputs may be any that keep to these rules, and one draw needn't show every extreme that they name: `frame_lengths`: the 4 utterance lengths of each micro-batch and group sum to 256. `token_lengths`: the 4 token counts of each micro-batch and group sum to 64.
All inputs are finite; a program needn't handle non-finite values.
Results may differ from a plain program's by a relative error of at most 0.04.
Values may be sent and summed in bfloat16 or wider, within the bound.
No kernel may reach another device: no remote copies, remote signals or barrier semaphores. Data moves between devices by JAX's collectives and lax.ppermute only.
A program may use at most 64 MiB of HBM per device.

v0:
```python
import math
import jax
import jax.numpy as jnp
from jax import lax
from jax.sharding import PartitionSpec as P

HS = 64
EPSILON = 1e-05
ROWS_DIMS = (((0,), (0,)), ((), ()))
FEAT_DIMS = (((1,), (1,)), ((), ()))


def partner(shard, axis, apart):
    return lax.ppermute(shard, axis, [(i, i ^ 1 << apart) for i in range(lax.axis_size(axis))])


def layer_norm(values, norm_gain, offset):
    center = values - jnp.mean(values, axis=-1, keepdims=True)
    variance = jnp.mean(center * center, axis=-1, keepdims=True)
    return center * lax.rsqrt(variance + EPSILON) * norm_gain + offset


def norm_backward(grad_out, values, norm_gain):
    center = values - jnp.mean(values, axis=-1, keepdims=True)
    variance = jnp.mean(center * center, axis=-1, keepdims=True)
    inverse = lax.rsqrt(variance + EPSILON)
    normed = center * inverse
    scaled = grad_out * norm_gain
    return inverse * (
        scaled
        - jnp.mean(scaled, axis=-1, keepdims=True)
        - normed * jnp.mean(scaled * normed, axis=-1, keepdims=True)
    )


def utterance_ids(lengths, row_count):
    bounds = jnp.cumsum(lengths, axis=1, dtype=jnp.int32)
    places = jnp.arange(row_count, dtype=jnp.int32)
    local_ids = jnp.sum((places[None, :, None] >= bounds[:, None, :]).astype(jnp.int32), axis=2)
    offsets = jnp.arange(lengths.shape[0], dtype=jnp.int32)[:, None] * lengths.shape[1]
    return (local_ids + offsets).reshape(-1)


def project(row_block, matrix):
    return lax.dot_general(row_block, matrix, FEAT_DIMS, preferred_element_type=jnp.float32).astype(
        jnp.bfloat16
    )


def outer_rows(left_rows, right_rows):
    return lax.dot_general(left_rows, right_rows, ROWS_DIMS, preferred_element_type=jnp.float32)


def split_heads(row_block):
    return row_block.reshape(row_block.shape[0], -1, HS)


def attend(queries, key_rows, value_rows, allowed):
    scaling = 1.0 / math.sqrt(HS)
    scores = (
        jnp.einsum(
            "qhd,khd->hqk",
            split_heads(queries),
            split_heads(key_rows),
            preferred_element_type=jnp.float32,
        )
        * scaling
    )
    scores = jnp.where(allowed[None], scores, -1e30)
    highest = jnp.max(scores, axis=-1, keepdims=True)
    raised = jnp.exp(scores - highest)
    attn_probs = raised / jnp.sum(raised, axis=-1, keepdims=True)
    context = jnp.einsum(
        "hqk,khd->qhd",
        attn_probs.astype(jnp.bfloat16),
        split_heads(value_rows),
        preferred_element_type=jnp.float32,
    )
    return (context.reshape(queries.shape[0], -1).astype(jnp.bfloat16), attn_probs)


def attend_backward(queries, key_rows, value_rows, attn_probs, grad_context):
    scaling = 1.0 / math.sqrt(HS)
    grad_heads = split_heads(grad_context)
    grad_probs = jnp.einsum(
        "qhd,khd->hqk", grad_heads, split_heads(value_rows), preferred_element_type=jnp.float32
    )
    grad_scores = (
        attn_probs * (grad_probs - jnp.sum(grad_probs * attn_probs, axis=-1, keepdims=True))
    ).astype(jnp.bfloat16)
    key_grad = (
        jnp.einsum(
            "hqk,qhd->khd", grad_scores, split_heads(queries), preferred_element_type=jnp.float32
        )
        * scaling
    )
    key_grad = key_grad.reshape(key_rows.shape[0], -1).astype(jnp.bfloat16)
    value_grad = jnp.einsum(
        "hqk,qhd->khd",
        attn_probs.astype(jnp.bfloat16),
        grad_heads,
        preferred_element_type=jnp.float32,
    )
    value_grad = value_grad.reshape(key_rows.shape[0], -1).astype(jnp.bfloat16)
    return (key_grad, value_grad)


def shards(
    frames, dec_states, out_grad, frame_lengths, token_lengths, weights, norm_gains, norm_biases
):
    is_encoder = lax.axis_index("segment") == 0
    matrices = weights[0]
    micro_count = frames.shape[0]
    shard_rows = frames.shape[1]
    features = frames.shape[2]
    head_cols = matrices.shape[1]
    head_count = head_cols // HS
    frame_count = shard_rows * lax.axis_size("mp")
    token_count = dec_states.shape[1]
    unit_count = micro_count // micro_count
    unit_rows = micro_count * frame_count
    received = jnp.zeros((micro_count, shard_rows, features), jnp.bfloat16)

    def empty_state():
        return (
            jnp.zeros((unit_rows, features), jnp.bfloat16),
            jnp.zeros((unit_rows, head_cols), jnp.bfloat16),
            jnp.zeros((unit_rows, head_cols), jnp.bfloat16),
            jnp.zeros((unit_rows, head_cols), jnp.bfloat16),
            jnp.zeros((unit_rows, head_cols), jnp.bfloat16),
            jnp.zeros((head_count, unit_rows, unit_rows), jnp.float32),
        )

    stored = {}
    totals = jnp.zeros((3, head_cols, features), jnp.float32)
    for moment in range(unit_count + 2):
        run_enc = moment < unit_count
        run_dec = 1 <= moment <= unit_count
        run_back = moment >= 2
        if run_enc:
            inputs = frames
        else:
            inputs = jnp.zeros((micro_count, shard_rows, features), jnp.bfloat16)
        enc_full, dec_full = (
            lax.all_gather(inputs, "mp", axis=1, tiled=True),
            lax.all_gather(received, "mp", axis=1, tiled=True),
        )

        def encoder_part():
            partial_value = jnp.zeros((unit_rows, features), jnp.float32)
            grad_step = jnp.zeros((3, head_cols, features), jnp.float32)
            saved_state = empty_state()
            if run_enc:
                lengths = frame_lengths[moment * micro_count : (moment + 1) * micro_count, 0]
                frame_ids = utterance_ids(lengths, frame_count)
                row_input = enc_full.reshape(unit_rows, features)
                normed = layer_norm(
                    row_input.astype(jnp.float32), norm_gains[0], norm_biases[0]
                ).astype(jnp.bfloat16)
                queries = project(normed, matrices[0])
                key_rows = project(normed, matrices[1])
                value_rows = project(normed, matrices[2])
                context, attn_probs = attend(
                    queries, key_rows, value_rows, frame_ids[:, None] == frame_ids[None, :]
                )
                partial_value = jnp.dot(context, matrices[3], preferred_element_type=jnp.float32)
                saved_state = (normed, queries, key_rows, value_rows, context, attn_probs)
            if run_back:
                normed_old, queries_old, keys_old, values_old, context_old, probs_old = stored[
                    moment - 2
                ]
                grad_rows = dec_full.reshape(unit_rows, features)
                out_weight_grad = outer_rows(context_old, grad_rows)
                grad_context = project(grad_rows, matrices[3])
                key_grad, value_grad = attend_backward(
                    queries_old, keys_old, values_old, probs_old, grad_context
                )
                grad_step = jnp.stack(
                    [
                        outer_rows(key_grad, normed_old),
                        outer_rows(value_grad, normed_old),
                        out_weight_grad,
                    ]
                )
            return (partial_value, grad_step, saved_state)

        def decoder_part():
            partial_value = jnp.zeros((unit_rows, features), jnp.float32)
            grad_step = jnp.zeros((3, head_cols, features), jnp.float32)
            if run_dec:
                batch_index = moment - 1
                first_micro = batch_index * micro_count
                frame_ids = utterance_ids(
                    frame_lengths[first_micro : first_micro + micro_count, 0], frame_count
                )
                token_ids = utterance_ids(
                    token_lengths[first_micro : first_micro + micro_count, 0], token_count
                )
                tokens = dec_states.reshape(micro_count * token_count, features)
                upstream = out_grad.reshape(micro_count * token_count, features)
                states_in = dec_full.reshape(unit_rows, features)
                normed = layer_norm(
                    states_in.astype(jnp.float32), norm_gains[2], norm_biases[2]
                ).astype(jnp.bfloat16)
                token_normed = layer_norm(
                    tokens.astype(jnp.float32), norm_gains[1], norm_biases[1]
                ).astype(jnp.bfloat16)
                queries = project(token_normed, matrices[0])
                key_rows = project(normed, matrices[1])
                value_rows = project(normed, matrices[2])
                context, attn_probs = attend(
                    queries, key_rows, value_rows, token_ids[:, None] == frame_ids[None, :]
                )
                grad_context = project(upstream, matrices[3])
                out_weight_grad = outer_rows(context, upstream)
                key_grad, value_grad = attend_backward(
                    queries, key_rows, value_rows, attn_probs, grad_context
                )
                grad_step = jnp.stack(
                    [outer_rows(key_grad, normed), outer_rows(value_grad, normed), out_weight_grad]
                )
                partial_value = jnp.dot(
                    key_grad, matrices[1], preferred_element_type=jnp.float32
                ) + jnp.dot(value_grad, matrices[2], preferred_element_type=jnp.float32)
            return (partial_value, grad_step, empty_state())

        partial_value, grad_step, saved_state = lax.cond(is_encoder, encoder_part, decoder_part)
        totals = totals + grad_step
        if run_enc:
            stored[moment] = saved_state
        if run_enc or run_dec:
            partial_value = partial_value.reshape(micro_count, frame_count, features)
            summed = lax.psum_scatter(
                partial_value.astype(jnp.bfloat16), "mp", scatter_dimension=1, tiled=True
            ).astype(jnp.float32)
            states_out = (inputs.astype(jnp.float32) + summed).astype(jnp.bfloat16)
            grads_out = norm_backward(summed, received.astype(jnp.float32), norm_gains[2]).astype(
                jnp.bfloat16
            )
            received = partner(jnp.where(is_encoder, states_out, grads_out), "segment", 0)
    gradient = lax.psum(totals.astype(jnp.bfloat16), "dp").astype(jnp.float32)
    return gradient[None]


def solution(mesh):
    placed = (
        P(None, ("dp", "mp"), None),
        P(None, "dp", None),
        P(None, "dp", None),
        P(None, "dp", None),
        P(None, "dp", None),
        P("segment", None, "mp", None),
        P(),
        P(),
    )
    return jax.shard_map(
        shards,
        mesh=mesh,
        in_specs=placed,
        out_specs=P("segment", None, "mp", None),
        check_vma=False,
    )
```

profile of v0, /device:TPU:16, one launch (start us, length us, event | category | flops | bytes accessed | tf_op | source)
XLA Modules:
  0.0 465.4 jit_solution(17567042108536954914)
XLA Ops:
  6.5 0.7 all-gather.4.cloned.1.call-update
  7.3 49.3 %all-gather.4.cloned.1.call-done = bf16[2,256,1280]{2,1,0:T(8,128)(2,1)} async-done(((bf16[2,32,1280]{2,1,0:T(8,128)(2,1)}), bf16[2,256,1280]{2,1,0:T(8,128)(2,1)}) %all-gather.4.cloned.1.call-update) | async-done | bytes 1310736 | tf_op jit(solution)/shard_map/all_gather | solution.py:145
  56.6 21.9 %conditional.3 = (bf16[512,1280]{1,0:T(8,128)(2,1)}, bf16[512,1280]{1,0:T(8,128)(2,1)}, bf16[512,128]{0,1:T(8,128)(2,1)}, bf16[512,128]{0,1:T(8,128)(2,1)S(1)}, ...) conditional(s32[]{:T(128)} %convert_element_type.217, () %tuple.34, ...), branch_computations={%region_0.0_spmd, %region_1.8_spmd} | conditional | flops 820780032 | bytes 47561236 | solution.py:227
  56.7 0.9 slice_reduce_fusion
  57.5 1.6 convert_reduce_fusion
  59.1 0.6 fusion.28
  59.7 0.5 multiply_reduce_fusion.1
  60.2 0.6 fusion.29
  60.8 0.6 add_convert_fusion
  61.4 1.5 convolution_convert_fusion.5
  63.5 2.2 convolution_convert_fusion.4
  65.7 1.5 convolution_convert_fusion.3
  67.2 3.8 fusion.87
  71.0 1.9 broadcast_divide_fusion
  72.9 1.3 convolution_convert_fusion.2
  74.2 2.7 fusion.15
  76.9 1.6 fusion.9
  78.6 0.8 slice_reduce_fusion.6
  79.4 40.5 %reduce-scatter.3.cloned.1.call-done = bf16[2,32,1280]{2,1,0:T(8,128)(2,1)} async-done(((bf16[2,256,1280]{2,1,0:T(8,128)(2,1)}), bf16[2,32,1280]{2,1,0:T(8,128)(2,1)}) %reduce-scatter.3.cloned.1.call-update) | async-done | bytes 163856 | tf_op jit(solution)/shard_map/reduce_scatter | solution.py:233
  119.9 1.0 fusion.69
  121.0 1.1 fusion.86
  122.1 1.9 collective-permute-start
  124.0 1.4 collective-permute-done
  125.4 0.7 copy-done.4
  126.1 40.7 %all-gather.6.cloned.1.call-done = bf16[2,256,1280]{2,1,0:T(8,128)(2,1)} async-done(((bf16[2,32,1280]{2,1,0:T(8,128)(2,1)}), bf16[2,256,1280]{2,1,0:T(8,128)(2,1)}) %all-gather.6.cloned.1.call-update) | async-done | bytes 1310736 | tf_op jit(solution)/shard_map/all_gather | solution.py:146
  166.8 2.6 conditional.4
  166.8 1.2 broadcast.393
  168.0 1.4 broadcast.394
  169.7 1.0 convert_reduce_fusion.6
  170.7 1.1 fusion.78
  171.8 66.8 %reduce-scatter.5.cloned.1.call-done = bf16[2,32,1280]{2,1,0:T(8,128)(2,1)} async-done(((bf16[2,256,1280]{2,1,0:T(8,128)(2,1)}), bf16[2,32,1280]{2,1,0:T(8,128)(2,1)}) %reduce-scatter.5.cloned.1.call-update) | async-done | bytes 163856 | tf_op jit(solution)/shard_map/reduce_scatter | solution.py:233
  238.6 1.2 fusion.84
  239.9 1.2 fusion.85
  241.0 1.9 collective-permute-start.1
  243.0 1.4 collective-permute-done.1
  244.3 0.7 copy-done.11
  245.1 40.9 %all-gather.8.cloned.1.call-done = bf16[2,256,1280]{2,1,0:T(8,128)(2,1)} async-done(((bf16[2,32,1280]{2,1,0:T(8,128)(2,1)}), bf16[2,256,1280]{2,1,0:T(8,128)(2,1)}) %all-gather.8.cloned.1.call-update) | async-done | bytes 1310736 | tf_op jit(solution)/shard_map/all_gather | solution.py:146
  285.9 9.2 %conditional.5 = (f32[3,128,1280]{2,1,0:T(8,128)S(1)}) conditional(s32[]{:T(128)} %convert_element_type.217, () %tuple.38, (bf16[2,256,1280]{2,1,0:T(8,128)(2,1)}, bf16[4,128,1280]{2,1,0:T(8,128)(2,1)}, bf16[512,128]{0,1:T(8,128)(2,1)S(1)}, f32[2,512,512]{1,2,0:T(8,128)S(1)}, bf16[512,128]{0,1:T(8,128)(2,1)}, ...), branch_computations={%region_29.30_spmd, %region_30.32_spmd} | conditional | flops 876805120 | bytes 28516388 | solution.py:227
  285.9 1.8 convolution_bitcast_fusion
  287.8 1.5 convolution_convert_fusion.1
  289.3 0.4 convolution_convert_fusion
  289.8 1.7 convolution_bitcast_fusion.1
  291.4 0.5 multiply_reduce_fusion
  291.9 1.4 fusion
  293.3 1.7 convolution_bitcast_fusion.2
  295.1 2.7 fusion.66
  297.9 158.0 %all-reduce.2.cloned.1.call-done = bf16[1,3,128,1280]{3,2,1,0:T(8,128)(2,1)} async-done(((bf16[1,3,128,1280]{3,2,1,0:T(8,128)(2,1)}), bf16[1,3,128,1280]{3,2,1,0:T(8,128)(2,1)}) %all-reduce.2.cloned.1.call-update) | async-done | bytes 983056 | tf_op jit(solution)/shard_map/psum | solution.py:241
  455.9 2.6 broadcast_in_dim.37
  (55 shorter events, 1.3 us)
Async XLA Ops:
  6.5 50.1 %all-gather.4.cloned.1.call-start = ((), (), s32[]{:S(2)}) async-start(), calls=%async_computation.2 | async-start | bytes 1474560 | tf_op jit(solution)/shard_map/all_gather | solution.py:145
  7.3 112.6 %reduce-scatter.3.cloned.1.call-start = ((), (), s32[]{:S(2)}) async-start(), calls=%async_computation.3 | async-start | bytes 1474560 | tf_op jit(solution)/shard_map/reduce_scatter | solution.py:233
  56.6 3.1 copy-start.2
  60.8 2.1 copy-start.17
  62.9 10.0 %copy-start.8 = (bf16[512,128]{0,1:T(8,128)(2,1)}, bf16[512,128]{0,1:T(8,128)(2,1)S(1)}, u32[]{:S(2)}) copy-start(bf16[512,128]{0,1:T(8,128)(2,1)S(1)} %convolution_convert_fusion.5) | copy-start | bytes 393220 | tf_op jit(solution)/shard_map/cond
  72.9 4.0 copy-start
  72.9 3.9 copy-start.15
  72.9 4.0 copy-start.14
  74.2 4.3 copy-start.9
  76.8 1.7 copy-start.1
  78.5 88.3 %copy-start.6 = (bf16[2,64,1280]{2,1,0:T(8,128)(2,1)S(1)}, bf16[2,64,1280]{2,1,0:T(8,128)(2,1)}, u32[]{:S(2)}) copy-start(bf16[2,64,1280]{2,1,0:T(8,128)(2,1)} %param.15) | copy-start | bytes 983044
  78.5 88.3 %copy-start.12 = (f32[3,1280]{1,0:T(4,128)S(1)}, f32[3,1280]{1,0:T(4,128)}, u32[]{:S(2)}) copy-start(f32[3,1280]{1,0:T(4,128)} %param.20) | copy-start | bytes 46084
  78.5 88.3 %copy-start.13 = (f32[3,1280]{1,0:T(4,128)S(1)}, f32[3,1280]{1,0:T(4,128)}, u32[]{:S(2)}) copy-start(f32[3,1280]{1,0:T(4,128)} %param.21) | copy-start | bytes 46084
  78.5 88.3 %copy-start.16 = (s32[2,1,4]{2,1,0:T(1,128)S(1)}, s32[2,1,4]{2,1,0:T(1,128)}, u32[]{:S(2)}) copy-start(s32[2,1,4]{2,1,0:T(1,128)} %param.17) | copy-start | bytes 100
  78.6 88.2 %all-gather.6.cloned.1.call-start = ((), (), s32[]{:S(2)}) async-start(), calls=%async_computation.4 | async-start | bytes 1474560 | tf_op jit(solution)/shard_map/all_gather | solution.py:146
  122.1 3.3 collective-permute-start
  125.4 0.7 copy-start.4
  126.1 112.6 %reduce-scatter.5.cloned.1.call-start = ((), (), s32[]{:S(2)}) async-start(), calls=%async_computation.5 | async-start | bytes 1474560 | tf_op jit(solution)/shard_map/reduce_scatter | solution.py:233
  169.4 70.4 %copy-start.5 = (bf16[2,32,1280]{2,1,0:T(8,128)(2,1)S(1)}, bf16[2,32,1280]{2,1,0:T(8,128)(2,1)}, u32[]{:S(2)}) copy-start(bf16[2,32,1280]{2,1,0:T(8,128)(2,1)} %copy-done.4) | copy-start | bytes 491524
  169.5 116.5 %all-gather.8.cloned.1.call-start = ((), (), s32[]{:S(2)}) async-start(), calls=%async_computation.6 | async-start | bytes 1474560 | tf_op jit(solution)/shard_map/all_gather | solution.py:146
  241.0 3.3 collective-permute-start.1
  244.3 0.7 copy-start.11
  245.0 210.9 %all-reduce.2.cloned.1.call-start = ((), (), s32[]{:S(2)}) async-start(), calls=%async_computation.7 | async-start | bytes 1966080 | tf_op jit(solution)/shard_map/psum | solution.py:241
  285.9 1.8 copy-start.7
Sparse Core Ops, SparseCore 0:
  9.4 47.1 all-gather.3
  78.7 41.1 reduce-scatter.2
  126.2 40.5 all-gather.5
  169.6 68.9 reduce-scatter.4
  245.1 40.7 all-gather.7
  298.0 157.8 all-reduce.1
where the time goes:
time: 466 us; the launch traced here: 465 us
  waiting for transfers between devices  400 us (86%)
  matrix products  21.9 us (5%)
  other arithmetic  20.1 us (4%)
  between operations  13.6 us (3%)
  local copies, waits for them, and re-layouts  5.66 us (1%)
    psum x1, waiting for transfers between devices, shards(): gradient = lax.psum(totals.astype(jnp.bfloat16), 'dp').astype(jnp.float32)  158 us
    reduce_scatter x2, waiting for transfers between devices, shards(): lax.psum_scatter(partial_value.astype(jnp.bfloat16), 'mp', scatter_dimens...  107 us
    all_gather x2, waiting for transfers between devices, shards(): lax.all_gather(received, 'mp', axis=1, tiled=True)  81.6 us
    all_gather x1, waiting for transfers between devices, shards(): lax.all_gather(inputs, 'mp', axis=1, tiled=True)  49.3 us
  transfers between devices with their start and end apart: 8, of which 8 were waited for; matrix products, arithmetic and copies ran while one was open for 1% of the time, Pallas kernels for 0%

commit v1 on v0

--- a/solution.py
+++ b/solution.py
@@ -238,7 +238,9 @@
                 jnp.bfloat16
             )
             received = partner(jnp.where(is_encoder, states_out, grads_out), "segment", 0)
-    gradient = lax.psum(totals.astype(jnp.bfloat16), "dp").astype(jnp.float32)
+    gradient = jnp.sum(lax.all_gather(totals.astype(jnp.bfloat16), "dp"), axis=0).astype(
+        jnp.float32
+    )
     return gradient[None]
 
 

time: 466 us -> 522 us (1.12)
  the two profiles are of different devices: /device:TPU:16 before, /device:TPU:1 now
where the time goes in v1:
time: 522 us; the launch traced here: 521 us
  waiting for transfers between devices  450 us (86%)
  other arithmetic  24.2 us (5%)
  starting transfers between devices  13.9 us (3%)
  between operations  13.6 us (3%)
  local copies, waits for them, and re-layouts  11 us (2%)
  matrix products  8.14 us (2%)
    all_gather x1, waiting for transfers between devices, shards(): lax.all_gather(totals.astype(jnp.bfloat16), 'dp')  239 us
    reduce_scatter x2, waiting for transfers between devices, shards(): lax.psum_scatter(partial_value.astype(jnp.bfloat16), 'mp', scatter_dimens...  90.3 us
    all_gather x2, waiting for transfers between devices, shards(): lax.all_gather(received, 'mp', axis=1, tiled=True)  72.2 us
    all_gather x1, waiting for transfers between devices, shards(): lax.all_gather(inputs, 'mp', axis=1, tiled=True)  45.8 us
    ppermute x2, starting transfers between devices, partner(): lax.ppermute(shard, axis, [(i, i ^ 1 << apart) for i in range(lax.axis_si...  13.5 us
    reduce_sum x1, other arithmetic, shards(): jnp.sum(lax.all_gather(totals.astype(jnp.bfloat16), 'dp'), axis=0)  11.1 us
  transfers between devices with their start and end apart: 8, of which 8 were waited for; matrix products, arithmetic and copies ran while one was open for 0% of the time, Pallas kernels for 0%

profile of v1, /device:TPU:1, one launch (start us, length us, event | category | flops | bytes accessed | tf_op | source)
XLA Modules:
  0.0 521.0 jit_solution(14301972151272070039)
XLA Ops:
  6.5 0.7 all-gather.6.cloned.1.call-update
  7.3 45.8 %all-gather.6.cloned.1.call-done = bf16[2,256,1280]{2,1,0:T(8,128)(2,1)} async-done(((bf16[2,32,1280]{2,1,0:T(8,128)(2,1)}), bf16[2,256,1280]{2,1,0:T(8,128)(2,1)}) %all-gather.6.cloned.1.call-update) | async-done | bytes 1310736 | tf_op jit(solution)/shard_map/all_gather | solution.py:145
  53.1 4.8 conditional.3
  53.1 1.1 broadcast.378
  54.3 1.6 broadcast.381
  55.9 0.6 broadcast.380.clone.1
  56.5 0.7 broadcast.380.clone
  57.2 0.7 broadcast.380
  58.1 1.3 slice_reduce_fusion.6
  59.4 53.9 %reduce-scatter.3.cloned.1.call-done = bf16[2,32,1280]{2,1,0:T(8,128)(2,1)} async-done(((bf16[2,256,1280]{2,1,0:T(8,128)(2,1)}), bf16[2,32,1280]{2,1,0:T(8,128)(2,1)}) %reduce-scatter.3.cloned.1.call-update) | async-done | bytes 163856 | tf_op jit(solution)/shard_map/reduce_scatter | solution.py:233
  113.3 1.0 fusion.68
  114.4 1.1 fusion.85
  115.5 6.9 %collective-permute-start = (bf16[2,32,1280]{2,1,0:T(8,128)(2,1)S(1)}, bf16[2,32,1280]{2,1,0:T(8,128)(2,1)S(1)}, u32[]{:S(2)}, u32[]{:S(2)}) collective-permute-start(bf16[2,32,1280]{2,1,0:T(8,128)(2,1)S(1)} %fusion.85), channel_id=1, source_target_pairs={{0,8},{8,0},{1,9},{9,1},{2,10},{10,2},{3,11},{11,3},{4,12},{12,4},... | collective-permute-start | bytes 491528 | tf_op jit(solution)/shard_map/ppermute | solution.py:14
  122.4 1.0 collective-permute-done
  123.4 0.7 copy-done.4
  124.2 36.1 %all-gather.8.cloned.1.call-done = bf16[2,256,1280]{2,1,0:T(8,128)(2,1)} async-done(((bf16[2,32,1280]{2,1,0:T(8,128)(2,1)}), bf16[2,256,1280]{2,1,0:T(8,128)(2,1)}) %all-gather.8.cloned.1.call-update) | async-done | bytes 1310736 | tf_op jit(solution)/shard_map/all_gather | solution.py:146
  160.3 14.6 %conditional.4 = (bf16[512,1280]{1,0:T(8,128)(2,1)}, f32[3,128,1280]{2,1,0:T(8,128)S(1)}) conditional(s32[]{:T(128)} %convert_element_type.231, (bf16[2,64,1280]{2,1,0:T(8,128)(2,1)S(1)}, f32[3,1280]{1,0:T(4,128)S(1)}, f32[3,1280]{1,0:T(4,128)S(1)}, bf16[4,128,1280]{2,1,0:T(8,128)(2,1)}, s32[2,1,4]{2,1,0:T(1,128)S(1)}, ...), branch_computations={%region_11.23_spmd, %region_23.24_spmd} | conditional | flops 1282403072 | bytes 51815376 | solution.py:227
  161.5 1.6 convert_reduce_fusion.2
  163.1 0.5 fusion.33
  163.9 0.6 fusion.36
  164.6 0.6 convolution_convert_fusion.7
  165.1 0.6 convolution_convert_fusion.8
  165.7 0.3 fusion.46
  166.2 0.4 fusion.87
  166.7 1.1 multiply_reduce_fusion.2
  167.7 0.7 convolution_convert_fusion.11
  168.4 0.3 copy-done.23
  168.8 0.7 fusion.40
  169.5 0.6 convolution_convert_fusion.6
  170.3 0.3 convolution_bitcast_fusion.5
  170.7 0.3 convolution_bitcast_fusion.4
  171.3 1.1 copy-done.10
  172.4 0.5 fusion.50
  172.9 0.4 copy-done.14
  173.3 1.6 convolution_add_fusion
  175.5 36.5 %reduce-scatter.5.cloned.1.call-done = bf16[2,32,1280]{2,1,0:T(8,128)(2,1)} async-done(((bf16[2,256,1280]{2,1,0:T(8,128)(2,1)}), bf16[2,32,1280]{2,1,0:T(8,128)(2,1)}) %reduce-scatter.5.cloned.1.call-update) | async-done | bytes 163856 | tf_op jit(solution)/shard_map/reduce_scatter | solution.py:233
  212.0 1.1 fusion.83
  213.1 1.2 fusion.84
  214.3 6.6 %collective-permute-start.1 = (bf16[2,32,1280]{2,1,0:T(8,128)(2,1)S(1)}, bf16[2,32,1280]{2,1,0:T(8,128)(2,1)S(1)}, u32[]{:S(2)}, u32[]{:S(2)}) collective-permute-start(bf16[2,32,1280]{2,1,0:T(8,128)(2,1)S(1)} %fusion.84), channel_id=1, source_target_pairs={{0,8},{8,0},{1,9},{9,1},{2,10},{10,2},{3,11},{11,3},{4,12},{12,4},... | collective-permute-start | bytes 491528 | tf_op jit(solution)/shard_map/ppermute | solution.py:14
  220.9 1.0 collective-permute-done.1
  221.9 0.7 copy-done.18
  222.7 36.1 %all-gather.10.cloned.1.call-done = bf16[2,256,1280]{2,1,0:T(8,128)(2,1)} async-done(((bf16[2,32,1280]{2,1,0:T(8,128)(2,1)}), bf16[2,256,1280]{2,1,0:T(8,128)(2,1)}) %all-gather.10.cloned.1.call-update) | async-done | bytes 1310736 | tf_op jit(solution)/shard_map/all_gather | solution.py:146
  258.8 1.4 conditional.5
  258.8 1.4 broadcast.395
  260.2 2.7 add_convert_fusion.1
  263.0 238.8 %all-gather.12.cloned.1.call-done = bf16[96,128,1280]{2,1,0:T(8,128)(2,1)} async-done(((bf16[3,128,1280]{2,1,0:T(8,128)(2,1)}), bf16[96,128,1280]{2,1,0:T(8,128)(2,1)}) %all-gather.12.cloned.1.call-update) | async-done | bytes 31457296 | tf_op jit(solution)/shard_map/all_gather | solution.py:241
  501.7 11.1 %reduce_sum.199 = bf16[3,128,1280]{2,1,0:T(8,128)(2,1)S(1)} reduce(bf16[32,3,128,1280]{3,2,1,0:T(8,128)(2,1)} %bitcast.154, bf16[]{:T(256)} %constant.111.clone.1), dimensions={0}, to_apply=%region_32.33 | reduce | flops 15237120 | bytes 32440322 | tf_op jit(solution)/shard_map/reduce_sum | solution.py:241
  512.8 1.4 bitcast_convert_fusion
  (73 shorter events, 3.2 us)
Async XLA Ops:
  6.5 46.6 %all-gather.6.cloned.1.call-start = ((), (), s32[]{:S(2)}) async-start(), calls=%async_computation.2 | async-start | bytes 1474560 | tf_op jit(solution)/shard_map/all_gather | solution.py:145
  7.3 106.1 %reduce-scatter.3.cloned.1.call-start = ((), (), s32[]{:S(2)}) async-start(), calls=%async_computation.3 | async-start | bytes 1474560 | tf_op jit(solution)/shard_map/reduce_scatter | solution.py:233
  57.9 102.3 %copy-start.2 = (bf16[512,1280]{1,0:T(8,128)(2,1)}, bf16[512,1280]{1,0:T(8,128)(2,1)S(1)}, u32[]{:S(2)}) copy-start(bf16[512,1280]{1,0:T(8,128)(2,1)S(1)} %get-tuple-element.111) | copy-start | bytes 3932164
  57.9 102.3 %copy-start.6 = (bf16[2,64,1280]{2,1,0:T(8,128)(2,1)S(1)}, bf16[2,64,1280]{2,1,0:T(8,128)(2,1)}, u32[]{:S(2)}) copy-start(bf16[2,64,1280]{2,1,0:T(8,128)(2,1)} %param.15) | copy-start | bytes 983044
  58.0 102.3 %copy-start.17 = (bf16[2,64,1280]{2,1,0:T(8,128)(2,1)S(1)}, bf16[2,64,1280]{2,1,0:T(8,128)(2,1)}, u32[]{:S(2)}) copy-start(bf16[2,64,1280]{2,1,0:T(8,128)(2,1)} %param.16) | copy-start | bytes 983044
  58.0 102.3 %copy-start.19 = (f32[3,1280]{1,0:T(4,128)S(1)}, f32[3,1280]{1,0:T(4,128)}, u32[]{:S(2)}) copy-start(f32[3,1280]{1,0:T(4,128)} %param.20) | copy-start | bytes 46084
  58.0 102.2 %copy-start.20 = (f32[3,1280]{1,0:T(4,128)S(1)}, f32[3,1280]{1,0:T(4,128)}, u32[]{:S(2)}) copy-start(f32[3,1280]{1,0:T(4,128)} %param.21) | copy-start | bytes 46084
  58.0 102.2 %copy-start.21 = (s32[2,1,4]{2,1,0:T(1,128)S(1)}, s32[2,1,4]{2,1,0:T(1,128)}, u32[]{:S(2)}) copy-start(s32[2,1,4]{2,1,0:T(1,128)} %param.17) | copy-start | bytes 100
  58.0 102.2 %copy-start.22 = (s32[2,1,4]{2,1,0:T(1,128)S(1)}, s32[2,1,4]{2,1,0:T(1,128)}, u32[]{:S(2)}) copy-start(s32[2,1,4]{2,1,0:T(1,128)} %param.18) | copy-start | bytes 100
  58.0 102.2 %all-gather.8.cloned.1.call-start = ((), (), s32[]{:S(2)}) async-start(), calls=%async_computation.4 | async-start | bytes 1474560 | tf_op jit(solution)/shard_map/all_gather | solution.py:146
  115.5 7.9 %collective-permute-start = (bf16[2,32,1280]{2,1,0:T(8,128)(2,1)S(1)}, bf16[2,32,1280]{2,1,0:T(8,128)(2,1)S(1)}, u32[]{:S(2)}, u32[]{:S(2)}) collective-permute-start(bf16[2,32,1280]{2,1,0:T(8,128)(2,1)S(1)} %fusion.85), channel_id=1, source_target_pairs={{0,8},{8,0},{1,9},{9,1},{2,10},{10,2},{3,11},{11,3},{4,12},{12,4},... | collective-permute-start | bytes 491528 | tf_op jit(solution)/shard_map/ppermute | solution.py:14
  123.4 0.7 copy-start.4
  124.1 87.8 %reduce-scatter.5.cloned.1.call-start = ((), (), s32[]{:S(2)}) async-start(), calls=%async_computation.5 | async-start | bytes 1474560 | tf_op jit(solution)/shard_map/reduce_scatter | solution.py:233
  160.3 14.9 %copy-start.5 = (bf16[2,32,1280]{2,1,0:T(8,128)(2,1)S(1)}, bf16[2,32,1280]{2,1,0:T(8,128)(2,1)}, u32[]{:S(2)}) copy-start(bf16[2,32,1280]{2,1,0:T(8,128)(2,1)} %copy-done.4) | copy-start | bytes 491524
  160.3 2.8 copy-start.1
  161.1 2.5 copy-start.9
  167.7 1.0 copy-start.23
  169.5 1.2 copy-start.11
  170.1 0.6 copy-start.13
  171.1 1.3 copy-start.10
  171.1 1.3 copy-start.12
  172.4 0.9 copy-start.14
  174.9 83.9 %copy-start.3 = (bf16[512,1280]{1,0:T(8,128)(2,1)S(1)}, bf16[512,1280]{1,0:T(8,128)(2,1)}, u32[]{:S(2)}) copy-start(bf16[512,1280]{1,0:T(8,128)(2,1)} %copy-done.2) | copy-start | bytes 3932164
  174.9 83.8 %all-gather.10.cloned.1.call-start = ((), (), s32[]{:S(2)}) async-start(), calls=%async_computation.6 | async-start | bytes 1474560 | tf_op jit(solution)/shard_map/all_gather | solution.py:146
  214.3 7.7 %collective-permute-start.1 = (bf16[2,32,1280]{2,1,0:T(8,128)(2,1)S(1)}, bf16[2,32,1280]{2,1,0:T(8,128)(2,1)S(1)}, u32[]{:S(2)}, u32[]{:S(2)}) collective-permute-start(bf16[2,32,1280]{2,1,0:T(8,128)(2,1)S(1)} %fusion.84), channel_id=1, source_target_pairs={{0,8},{8,0},{1,9},{9,1},{2,10},{10,2},{3,11},{11,3},{4,12},{12,4},... | collective-permute-start | bytes 491528 | tf_op jit(solution)/shard_map/ppermute | solution.py:14
  221.9 0.7 copy-start.18
  222.6 279.1 %all-gather.12.cloned.1.call-start = ((), (), s32[]{:S(2)}) async-start(), calls=%async_computation.7 | async-start | bytes 32440320 | tf_op jit(solution)/shard_map/all_gather | solution.py:241
Sparse Core Ops, SparseCore 0:
  9.4 43.6 all-gather.5
  58.2 55.1 reduce-scatter.2
  124.2 35.9 all-gather.7
  175.1 36.8 reduce-scatter.4
  222.7 35.9 all-gather.9
  263.1 238.5 all-gather.11
